TPU v7x, 32 devices: a whole 2x2x4 slice. The times are simulated.
32 devices in a mesh: snap: 4 (over z), vert: 8 (over y, x, core).
Axes of the slice: x: 2, y: 2, z: 4, core: 2. Of those that a mesh axis runs over, the one named last changes fastest.
Arguments:
- features: bfloat16 [4, 6144, 128], P('snap', 'vert'), may hold values from -6 to 6
- adjacency_tiles: bfloat16 [4, 96, 128, 128], P('snap', 'vert'), may hold values from -0.375 to 0.375
- src_block: int32 [4, 96], P('snap', 'vert'), may hold values from 0 to 47, as said below
- dst_block: int32 [4, 96], P('snap', 'vert'), may hold values from 0 to 5
- block_count: int32 [4, 8], P('snap', 'vert'), may hold values from 6 to 12, as said below
- w_conv: bfloat16 [128, 512], replicated, may hold values from -0.5 to 0.5
- b_conv: float32 [512], replicated, may hold values from -3 to 3
- w_input: bfloat16 [512, 2048], replicated, may hold values from -0.25 to 0.25
- w_state: bfloat16 [512, 2048], replicated, may hold values from -0.25 to 0.25
- b_gates: float32 [2048], replicated, may hold values from -3 to 3
Outputs:
- hidden_seq: bfloat16 [4, 6144, 512], P('snap', 'vert')
Inputs may be any that keep to these rules, and one draw needn't show every extreme that they name: `src_block`: slot s of owner v names a column block held by owner v - 1, v or v + 1 (clipped to the owners that exist); its first slot names one of owner v - 1 and its second one of owner v + 1 where those exist. `block_count`: in every snapshot some owner has all 12 slots live.
All inputs are finite; a program needn't handle non-finite values.
Results may differ from a plain program's by a relative error of at most 0.0044.
Values may be sent and summed in bfloat16 or wider, within the bound.
No kernel may reach another device: no remote copies, remote signals or barrier semaphores. Data moves between devices by JAX's collectives and lax.ppermute only.
A program may use at most 64 MiB of HBM per device.

v0:
```python
import jax
import jax.numpy as jnp
from jax import lax
from jax.sharding import PartitionSpec as P

forget_bias = 2.0


def padded(cells, sides, width):
    for axis, dim in sides:
        count = lax.axis_size(axis)
        ends = count - 1
        head = lax.slice_in_dim(cells, 0, width, axis=dim)
        tail = lax.slice_in_dim(cells, cells.shape[dim] - width, cells.shape[dim], axis=dim)
        cells = jnp.concatenate(
            [
                lax.ppermute(tail, axis, [(i, (i + 1) % count) for i in range(ends)]),
                cells,
                lax.ppermute(head, axis, [((i + 1) % count, i) for i in range(ends)]),
            ],
            axis=dim,
        )
    return cells


def gate_step(hidden, cell, pre_gates, w_state, b_gates):
    width = w_state.shape[0]
    gates = pre_gates + jnp.dot(hidden, w_state, preferred_element_type=jnp.float32) + b_gates
    input_gate = jax.nn.sigmoid(gates[:, :width])
    forget_gate = jax.nn.sigmoid(gates[:, width : 2 * width] + forget_bias)
    candidate = jnp.tanh(gates[:, 2 * width : 3 * width])
    output_gate = jax.nn.sigmoid(gates[:, 3 * width :])
    new_cell = forget_gate * cell + input_gate * candidate
    new_hidden = (output_gate * jnp.tanh(new_cell)).astype(jnp.bfloat16)
    return (new_hidden, new_cell)


def shards(
    features,
    adjacency_tiles,
    src_block,
    dst_block,
    block_count,
    w_conv,
    b_conv,
    w_input,
    w_state,
    b_gates,
):
    vert_rows = features.shape[1]
    feat_width = features.shape[2]
    block_rows = adjacency_tiles.shape[2]
    slot_count = adjacency_tiles.shape[1]
    row_blocks = vert_rows // block_rows
    hid_width = w_state.shape[0]
    owner_index = lax.axis_index("vert")
    window = padded(features, (("vert", 1),), vert_rows)
    window_blocks = window[0].reshape(3 * row_blocks, block_rows, feat_width)
    local_index = src_block[0] - (owner_index - 1) * row_blocks
    picked = jnp.take(window_blocks, local_index, axis=0)
    product = jnp.einsum(
        "ebk,ekf->ebf", adjacency_tiles[0], picked, preferred_element_type=jnp.float32
    )
    alive = jnp.arange(slot_count, dtype=jnp.int32) < block_count[0, 0]
    selector = (
        (dst_block[0][None, :] == jnp.arange(row_blocks, dtype=jnp.int32)[:, None]) & alive[None, :]
    ).astype(jnp.float32)
    summed = jnp.einsum("re,ebf->rbf", selector, product, precision=lax.Precision.HIGHEST)
    summed = summed.reshape(vert_rows, feat_width).astype(jnp.bfloat16)
    conv = jax.nn.relu(jnp.dot(summed, w_conv, preferred_element_type=jnp.float32) + b_conv).astype(
        jnp.bfloat16
    )
    regrouped = lax.all_to_all(conv[None], "snap", split_axis=1, concat_axis=0, tiled=True)
    pre_all = jnp.einsum("tvp,pg->tvg", regrouped, w_input, preferred_element_type=jnp.float32)
    slice_rows = regrouped.shape[1]

    def advance(carry, pre_now):
        hidden, cell = carry
        new_hidden, new_cell = gate_step(hidden, cell, pre_now, w_state, b_gates)
        return ((new_hidden, new_cell), new_hidden)

    start_state = (
        jnp.zeros((slice_rows, hid_width), jnp.bfloat16),
        jnp.zeros((slice_rows, hid_width), jnp.float32),
    )
    _, sequence = lax.scan(advance, start_state, pre_all)
    return lax.all_to_all(sequence, "snap", split_axis=0, concat_axis=1, tiled=True)


def solution(mesh):
    placed = (
        P("snap", "vert", None),
        P("snap", "vert", None, None),
        P("snap", "vert"),
        P("snap", "vert"),
        P("snap", "vert"),
        P(),
        P(),
        P(),
        P(),
        P(),
    )
    return jax.shard_map(
        shards, mesh=mesh, in_specs=placed, out_specs=P("snap", "vert", None), check_vma=False
    )
```

profile of v0, /device:TPU:4, one launch (start us, length us, event | category | flops | bytes accessed | tf_op | source)
XLA Modules:
  0.0 96.3 jit_solution(7456984444435545295)
XLA Ops:
  0.0 2.0 %collective-permute-start = (bf16[1,768,128]{2,1,0:T(8,128)(2,1)}, bf16[1,768,128]{2,1,0:T(8,128)(2,1)S(1)}, u32[]{:S(2)}, u32[]{:S(2)}) collective-permute-start(bf16[1,768,128]{2,1,0:T(8,128)(2,1)} %param.12), channel_id=1, source_target_pairs={{0,1},{1,2},{2,3},{3,4},{4,5},{5,6},{6,7},{8,9},{9,10},{10,11},{11... | collective-permute-start | bytes 589832 | tf_op jit(solution)/shard_map/ppermute | solution.py:17
  2.1 4.5 %collective-permute-start.1 = (bf16[1,768,128]{2,1,0:T(8,128)(2,1)}, bf16[1,768,128]{2,1,0:T(8,128)(2,1)S(1)}, u32[]{:S(2)}, u32[]{:S(2)}) collective-permute-start(bf16[1,768,128]{2,1,0:T(8,128)(2,1)} %param.12), channel_id=1, source_target_pairs={{1,0},{2,1},{3,2},{4,3},{5,4},{6,5},{7,6},{9,8},{10,9},{11,10},{12... | collective-permute-start | bytes 589832 | tf_op jit(solution)/shard_map/ppermute | solution.py:19
  6.6 0.7 fusion.32
  7.9 0.7 compare_and_fusion
  8.6 1.5 %collective-permute-done.1 = bf16[1,768,128]{2,1,0:T(8,128)(2,1)S(1)} collective-permute-done((bf16[1,768,128]{2,1,0:T(8,128)(2,1)}, bf16[1,768,128]{2,1,0:T(8,128)(2,1)S(1)}, u32[]{:S(2)}, u32[]{:S(2)}) %collective-permute-start.1) | collective-permute-done | bytes 196640 | tf_op jit(solution)/shard_map/ppermute | solution.py:19
  10.1 1.0 %pad_maximum_fusion = bf16[1,2304,128]{2,1,0:T(8,128)(2,1)S(1)} fusion(bf16[1,768,128]{2,1,0:T(8,128)(2,1)S(1)} %collective-permute-done.1, bf16[1,768,128]{2,1,0:T(8,128)(2,1)} %param.12, bf16[1,768,128]{2,1,0:T(8,128)(2,1)S(1)} %collective-permute-done), kind=kLoop, calls=%fused_computation.33 | loop fusion | flops 1769472 | bytes 1179648 | tf_op jit(solution)/shard_map/concatenate | solution.py:15
  11.1 0.6 gather_fusion
  11.7 1.4 %convolution_bitcast_fusion = f32[12,128,128]{1,2,0:T(8,128)} fusion(bf16[1,12,128,128]{3,2,1,0:T(8,128)(2,1)S(1)} %copy-done.2, bf16[12,128,128]{2,1,0:T(8,128)(2,1)S(1)} %gather_fusion, pred[12]{0:T(512)(128)(4,1)S(1)} %compare_and_fusion), kind=kOutput, calls=%fused_computation.31 | convolution fusion | flops 50528256 | bytes 1572876 | tf_op jit(solution)/shard_map/ebk,ekf->ebf/dot_general | solution.py:61
  13.1 1.7 %copy.16 = f32[12,128,128]{2,0,1:T(8,128)S(1)} copy(f32[12,128,128]{1,2,0:T(8,128)} %convolution_bitcast_fusion) | data formatting | bytes 1572864 | tf_op jit(solution)/shard_map/ebk,ekf->ebf/dot_general | solution.py:61
  15.7 2.4 %copy.22 = bf16[1,768,512]{2,0,1:T(2,128)(2,1)} copy(bf16[1,768,512]{2,1,0:T(8,128)(2,1)S(1)} %fusion.22) | data formatting | bytes 1572864 | tf_op jit(solution)/shard_map/broadcast_in_dim | solution.py:73
  18.6 6.4 %reduce = bf16[768,512]{1,0:T(8,128)(2,1)S(1)} reduce(bf16[768,1,512]{2,1,0:T(2,128)(2,1)} %bitcast.45, bf16[]{:T(256)} %broadcast.89), dimensions={1}, to_apply=%bitcast.37.reduce_sub_computation | reduce | bytes 1572866
  25.0 1.4 %reshape.53 = bf16[4,2,49152]{2,1,0:T(2,128)(2,1)} reshape(bf16[768,512]{1,0:T(8,128)(2,1)S(1)} %reduce) | data formatting | bytes 1572864
  26.4 4.9 %all-to-all-start = ((bf16[4,2,49152]{2,1,0:T(2,128)(2,1)}), bf16[4,2,49152]{2,1,0:T(2,128)(2,1)S(1)}, u32[]{:S(2)}, u32[]{:S(2)}) async-start(bf16[4,2,49152]{2,1,0:T(2,128)(2,1)} %reshape.53), calls=%async_computation | async-start | bytes 1572864 | tf_op jit(solution)/shard_map/all_to_all | solution.py:73
  31.3 21.0 %all-to-all-done = bf16[4,2,49152]{2,1,0:T(2,128)(2,1)S(1)} async-done(((bf16[4,2,49152]{2,1,0:T(2,128)(2,1)}), bf16[4,2,49152]{2,1,0:T(2,128)(2,1)S(1)}, u32[]{:S(2)}, u32[]{:S(2)}) %all-to-all-start) | async-done | bytes 786464 | tf_op jit(solution)/shard_map/all_to_all | solution.py:73
  52.3 2.1 %reshape.54 = bf16[768,1,512]{2,1,0:T(2,128)(2,1)} reshape(bf16[4,2,49152]{2,1,0:T(2,128)(2,1)S(1)} %all-to-all-done) | data formatting | bytes 1572864
  54.4 1.6 %copy.20 = bf16[1,768,512]{2,1,0:T(8,128)(2,1)S(1)} copy(bf16[1,768,512]{2,0,1:T(2,128)(2,1)} %bitcast.46) | data formatting | bytes 1572864
  56.0 4.5 %fusion.20 = f32[4,192,2048]{2,1,0:T(8,128)} fusion(bf16[4,192,512]{2,1,0:T(8,128)(2,1)S(1)} %bitcast.47, bf16[512,2048]{1,0:T(8,128)(2,1)S(1)} %copy-done), kind=kOutput, calls=%fused_computation.27 | convolution fusion | flops 1610612736 | bytes 9175040 | tf_op jit(solution)/shard_map/tvp,pg->tvg/dot_general | solution.py:74
  60.5 12.3 %while.15 = (s32[]{:T(128)}, bf16[192,512]{1,0:T(8,128)(2,1)S(1)}, f32[192,512]{1,0:T(8,128)S(1)}, bf16[4,192,512]{2,1,0:T(8,128)(2,1)S(1)}, f32[4,192,2048]{2,1...) while((s32[]{:T(128)}, bf16[192,512]{1,0:T(8,128)(2,1)S(1)}, ...), condition=%wide.region_1.2_spmd.clone, body=%wide.region_0.1_spmd.clone.sunk | while | flops 405110784 | bytes 8200304 | solution.py:86
  60.5 2.6 %fusion.46 = f32[192,2048]{1,0:T(8,128)S(1)} fusion(bf16[512,2048]{1,0:T(8,128)(2,1)} %get-tuple-element.156, f32[4,192,2048]{2,1,0:T(8,128)} %get-tuple-element.155, s32[]{:T(128)} %get-tuple-element.142, f32[2048]{0:T(1024)S(1)} %get-tuple-element.157, bf16[192,512]{1,0:T(8,128)(2,1)S(1)} %get-tuple-element.143, pred[]{:T(512)S(6)} %compare.3), kind=kOutput, calls=%fused_computation.2.clone.1 | convolution fusion | flops 403537920 | bytes 5447685 | tf_op jit(solution)/shard_map/while/body/eval_jaxpr/dot_general | solution.py:28
  63.5 2.6 %fusion.46 = f32[192,2048]{1,0:T(8,128)S(1)} fusion(bf16[512,2048]{1,0:T(8,128)(2,1)} %get-tuple-element.156, f32[4,192,2048]{2,1,0:T(8,128)} %get-tuple-element.155, s32[]{:T(128)} %get-tuple-element.142, f32[2048]{0:T(1024)S(1)} %get-tuple-element.157, bf16[192,512]{1,0:T(8,128)(2,1)S(1)} %get-tuple-element.143, pred[]{:T(512)S(6)} %compare.3), kind=kOutput, calls=%fused_computation.2.clone.1 | convolution fusion | flops 403537920 | bytes 5447685 | tf_op jit(solution)/shard_map/while/body/eval_jaxpr/dot_general | solution.py:28
  66.6 2.6 %fusion.46 = f32[192,2048]{1,0:T(8,128)S(1)} fusion(bf16[512,2048]{1,0:T(8,128)(2,1)} %get-tuple-element.156, f32[4,192,2048]{2,1,0:T(8,128)} %get-tuple-element.155, s32[]{:T(128)} %get-tuple-element.142, f32[2048]{0:T(1024)S(1)} %get-tuple-element.157, bf16[192,512]{1,0:T(8,128)(2,1)S(1)} %get-tuple-element.143, pred[]{:T(512)S(6)} %compare.3), kind=kOutput, calls=%fused_computation.2.clone.1 | convolution fusion | flops 403537920 | bytes 5447685 | tf_op jit(solution)/shard_map/while/body/eval_jaxpr/dot_general | solution.py:28
  69.7 2.6 %fusion.46 = f32[192,2048]{1,0:T(8,128)S(1)} fusion(bf16[512,2048]{1,0:T(8,128)(2,1)} %get-tuple-element.156, f32[4,192,2048]{2,1,0:T(8,128)} %get-tuple-element.155, s32[]{:T(128)} %get-tuple-element.142, f32[2048]{0:T(1024)S(1)} %get-tuple-element.157, bf16[192,512]{1,0:T(8,128)(2,1)S(1)} %get-tuple-element.143, pred[]{:T(512)S(6)} %compare.3), kind=kOutput, calls=%fused_computation.2.clone.1 | convolution fusion | flops 403537920 | bytes 5447685 | tf_op jit(solution)/shard_map/while/body/eval_jaxpr/dot_general | solution.py:28
  72.8 22.6 %all_to_all.24 = bf16[4,192,512]{2,1,0:T(8,128)(2,1)S(1)} all-to-all(bf16[4,192,512]{2,1,0:T(8,128)(2,1)S(1)} %get-tuple-element.42), channel_id=1, replica_groups=mesh['snap'=4,'vert'=8] {'snap'}, dimensions={0} | all-to-all | bytes 1572864 | tf_op jit(solution)/shard_map/all_to_all | solution.py:87
  95.4 0.9 copy.38
  (28 shorter events, 3.1 us)
Async XLA Ops:
  0.0 56.0 %copy-start = (bf16[512,2048]{1,0:T(8,128)(2,1)S(1)}, bf16[512,2048]{1,0:T(8,128)(2,1)}, u32[]{:S(2)}) copy-start(bf16[512,2048]{1,0:T(8,128)(2,1)} %param.19) | copy-start | bytes 6291460
  0.0 11.7 %copy-start.2 = (bf16[1,12,128,128]{3,2,1,0:T(8,128)(2,1)S(1)}, bf16[1,12,128,128]{3,2,1,0:T(8,128)(2,1)}, u32[]{:S(2)}) copy-start(bf16[1,12,128,128]{3,2,1,0:T(8,128)(2,1)} %param.13) | copy-start | bytes 1179652
  0.0 8.6 %collective-permute-start = (bf16[1,768,128]{2,1,0:T(8,128)(2,1)}, bf16[1,768,128]{2,1,0:T(8,128)(2,1)S(1)}, u32[]{:S(2)}, u32[]{:S(2)}) collective-permute-start(bf16[1,768,128]{2,1,0:T(8,128)(2,1)} %param.12), channel_id=1, source_target_pairs={{0,1},{1,2},{2,3},{3,4},{4,5},{5,6},{6,7},{8,9},{9,10},{10,11},{11... | collective-permute-start | bytes 589832 | tf_op jit(solution)/shard_map/ppermute | solution.py:17
  2.1 8.0 %collective-permute-start.1 = (bf16[1,768,128]{2,1,0:T(8,128)(2,1)}, bf16[1,768,128]{2,1,0:T(8,128)(2,1)S(1)}, u32[]{:S(2)}, u32[]{:S(2)}) collective-permute-start(bf16[1,768,128]{2,1,0:T(8,128)(2,1)} %param.12), channel_id=1, source_target_pairs={{1,0},{2,1},{3,2},{4,3},{5,4},{6,5},{7,6},{9,8},{10,9},{11,10},{12... | collective-permute-start | bytes 589832 | tf_op jit(solution)/shard_map/ppermute | solution.py:19
  11.7 3.1 %copy-start.6 = (s32[1,12]{1,0:T(1,128)S(1)}, s32[1,12]{1,0:T(1,128)}, u32[]{:S(2)}) copy-start(s32[1,12]{1,0:T(1,128)} %param.15) | copy-start | bytes 148
  13.1 2.2 %copy-start.4 = (bf16[128,512]{1,0:T(8,128)(2,1)S(1)}, bf16[128,512]{1,0:T(8,128)(2,1)}, u32[]{:S(2)}) copy-start(bf16[128,512]{1,0:T(8,128)(2,1)} %param.17) | copy-start | bytes 393220
  13.1 2.2 %copy-start.5 = (f32[512]{0:T(512)S(1)}, f32[512]{0:T(512)}, u32[]{:S(2)}) copy-start(f32[512]{0:T(512)} %param.18) | copy-start | bytes 6148
  26.4 25.9 %all-to-all-start = ((bf16[4,2,49152]{2,1,0:T(2,128)(2,1)}), bf16[4,2,49152]{2,1,0:T(2,128)(2,1)S(1)}, u32[]{:S(2)}, u32[]{:S(2)}) async-start(bf16[4,2,49152]{2,1,0:T(2,128)(2,1)} %reshape.53), calls=%async_computation | async-start | bytes 1572864 | tf_op jit(solution)/shard_map/all_to_all | solution.py:73
  56.0 4.5 %copy-start.1 = (bf16[4,192,512]{2,1,0:T(8,128)(2,1)S(1)}, bf16[4,192,512]{2,1,0:T(8,128)(2,1)}, u32[]{:S(2)}) copy-start(bf16[4,192,512]{2,1,0:T(8,128)(2,1)} %custom-call.4) | copy-start | bytes 2359300
  56.0 4.5 %copy-start.3 = (f32[2048]{0:T(1024)S(1)}, f32[2048]{0:T(1024)}, u32[]{:S(2)}) copy-start(f32[2048]{0:T(1024)} %param.21) | copy-start | bytes 24580
where the time goes:
time: 96.7 us; the launch traced here: 96.3 us
  blocking collectives  22.6 us (23%)
  waiting for transfers between devices  22.5 us (23%)
  matrix products  17.2 us (18%)
  starting transfers between devices  11.5 us (12%)
  local copies, waits for them, and re-layouts  11.1 us (11%)
  other arithmetic  10.4 us (11%)
    all_to_all x1, blocking collectives, shards(): lax.all_to_all(sequence, 'snap', split_axis=0, concat_axis=1, tiled=True)  22.6 us
    all_to_all x1, waiting for transfers between devices, shards(): lax.all_to_all(conv[None], 'snap', split_axis=1, concat_axis=0, tiled=True)  21 us
    dot_general x4, matrix products, gate_step(): jnp.dot(hidden, w_state, preferred_element_type=jnp.float32)  10.5 us
    unnamed x19, local copies, waits for them, and re-layouts  6.46 us
    unnamed x3, other arithmetic  6.4 us
    all_to_all x1, starting transfers between devices, shards(): lax.all_to_all(conv[None], 'snap', split_axis=1, concat_axis=0, tiled=True)  4.88 us
    ppermute x1, starting transfers between devices, padded(): lax.ppermute(head, axis, [((i + 1) % count, i) for i in range(ends)])  4.54 us
    dot_general x1, matrix products, shards(): jnp.einsum('tvp,pg->tvg', regrouped, w_input, preferred_element_type=jnp....  4.46 us
  transfers between devices with their start and end apart: 3, of which 2 were waited for; matrix products, arithmetic and copies ran while one was open for 1% of the time, Pallas kernels for 0%

commit v1 on v0

--- a/solution.py
+++ b/solution.py
@@ -70,7 +70,12 @@
     conv = jax.nn.relu(jnp.dot(summed, w_conv, preferred_element_type=jnp.float32) + b_conv).astype(
         jnp.bfloat16
     )
-    regrouped = lax.all_to_all(conv[None], "snap", split_axis=1, concat_axis=0, tiled=True)
+    regrouped = jnp.concatenate(
+        lax.all_to_all(
+            jnp.stack(jnp.split(conv[None], lax.axis_size("snap"), axis=1)), "snap", 0, 0
+        ),
+        axis=0,
+    )
     pre_all = jnp.einsum("tvp,pg->tvg", regrouped, w_input, preferred_element_type=jnp.float32)
     slice_rows = regrouped.shape[1]
 

time: 96.7 us -> 87 us (0.90)
  local copies, waits for them, and re-layouts: 11.1 us -> 3.27 us
  other arithmetic: 10.4 us -> 7.72 us
  blocking collectives: 22.6 us -> 23.6 us
    unnamed x3 -> x2, other arithmetic: 6.4 us -> 0.01 us
    unnamed x19 -> x13, local copies, waits for them, and re-layouts: 6.46 us -> 0.9 us
    dynamic_update_slice x4, other arithmetic: 1.71 us -> 4.42 us  [shards(): _, sequence = lax.scan(advance, start_state, pre_all)]
    broadcast_in_dim x1 -> x0, local copies, waits for them, and re-layouts: 2.37 us -> none  [shards(): conv[None]]
    all_to_all x1, blocking collectives: 22.6 us -> 23.6 us  [shards(): lax.all_to_all(sequence, 'snap', split_axis=0, concat_axis=1, tiled=True)]
    another operation x0 -> x1, other arithmetic: none -> 0.99 us  [shards(): jnp.stack(jnp.split(conv[None], lax.axis_size('snap'), axis=1))]
  transfers between devices with their start and end apart: 3 -> 3, of which waited for: 2 -> 2; matrix products, arithmetic and copies ran while one was open for 1% -> 2% of each run, Pallas kernels for 0% -> 0%
where the time goes in v1:
time: 87 us; the launch traced here: 86.6 us
  blocking collectives  23.6 us (27%)
  waiting for transfers between devices  22.5 us (26%)
  matrix products  17.2 us (20%)
  starting transfers between devices  11.5 us (13%)
  other arithmetic  7.72 us (9%)
  local copies, waits for them, and re-layouts  3.27 us (4%)
    all_to_all x1, blocking collectives, shards(): lax.all_to_all(sequence, 'snap', split_axis=0, concat_axis=1, tiled=True)  23.6 us
    all_to_all x1, waiting for transfers between devices, shards(): lax.all_to_all(jnp.stack(jnp.split(conv[None], lax.axis_size('snap'), axi...  21 us
    dot_general x4, matrix products, gate_step(): jnp.dot(hidden, w_state, preferred_element_type=jnp.float32)  10.5 us
    all_to_all x1, starting transfers between devices, shards(): lax.all_to_all(jnp.stack(jnp.split(conv[None], lax.axis_size('snap'), axi...  4.88 us
    ppermute x1, starting transfers between devices, padded(): lax.ppermute(head, axis, [((i + 1) % count, i) for i in range(ends)])  4.54 us
    dot_general x1, matrix products, shards(): jnp.einsum('tvp,pg->tvg', regrouped, w_input, preferred_element_type=jnp....  4.45 us
    dynamic_update_slice x4, other arithmetic, shards(): _, sequence = lax.scan(advance, start_state, pre_all)  4.42 us
    ppermute x1, starting transfers between devices, padded(): lax.ppermute(tail, axis, [(i, (i + 1) % count) for i in range(ends)])  2.04 us
  transfers between devices with their start and end apart: 3, of which 2 were waited for; matrix products, arithmetic and copies ran while one was open for 2% of the time, Pallas kernels for 0%

profile of v1, /device:TPU:4, one launch (start us, length us, event | category | flops | bytes accessed | tf_op | source)
XLA Modules:
  0.0 86.6 jit_solution(13449764888046697329)
XLA Ops:
  0.0 2.0 %collective-permute-start = (bf16[1,768,128]{2,1,0:T(8,128)(2,1)}, bf16[1,768,128]{2,1,0:T(8,128)(2,1)S(1)}, u32[]{:S(2)}, u32[]{:S(2)}) collective-permute-start(bf16[1,768,128]{2,1,0:T(8,128)(2,1)} %param.12), channel_id=1, source_target_pairs={{0,1},{1,2},{2,3},{3,4},{4,5},{5,6},{6,7},{8,9},{9,10},{10,11},{11... | collective-permute-start | bytes 589832 | tf_op jit(solution)/shard_map/ppermute | solution.py:17
  2.1 4.5 %collective-permute-start.1 = (bf16[1,768,128]{2,1,0:T(8,128)(2,1)}, bf16[1,768,128]{2,1,0:T(8,128)(2,1)S(1)}, u32[]{:S(2)}, u32[]{:S(2)}) collective-permute-start(bf16[1,768,128]{2,1,0:T(8,128)(2,1)} %param.12), channel_id=1, source_target_pairs={{1,0},{2,1},{3,2},{4,3},{5,4},{6,5},{7,6},{9,8},{10,9},{11,10},{12... | collective-permute-start | bytes 589832 | tf_op jit(solution)/shard_map/ppermute | solution.py:19
  6.6 0.7 fusion.35
  7.9 0.7 compare_and_fusion
  8.6 1.5 %collective-permute-done.1 = bf16[1,768,128]{2,1,0:T(8,128)(2,1)S(1)} collective-permute-done((bf16[1,768,128]{2,1,0:T(8,128)(2,1)}, bf16[1,768,128]{2,1,0:T(8,128)(2,1)S(1)}, u32[]{:S(2)}, u32[]{:S(2)}) %collective-permute-start.1) | collective-permute-done | bytes 196640 | tf_op jit(solution)/shard_map/ppermute | solution.py:19
  10.1 1.0 %pad_maximum_fusion.1 = bf16[1,2304,128]{2,1,0:T(8,128)(2,1)S(1)} fusion(bf16[1,768,128]{2,1,0:T(8,128)(2,1)S(1)} %collective-permute-done.1, bf16[1,768,128]{2,1,0:T(8,128)(2,1)} %param.12, bf16[1,768,128]{2,1,0:T(8,128)(2,1)S(1)} %collective-permute-done), kind=kLoop, calls=%fused_computation.35 | loop fusion | flops 1769472 | bytes 1179648 | tf_op jit(solution)/shard_map/concatenate | solution.py:15
  11.1 0.6 gather_fusion
  11.7 1.4 %fusion.25 = f32[12,128,128]{2,1,0:T(8,128)} fusion(bf16[1,12,128,128]{3,2,1,0:T(8,128)(2,1)S(1)} %copy-done.1, bf16[12,128,128]{2,1,0:T(8,128)(2,1)S(1)} %gather_fusion, pred[12]{0:T(512)(128)(4,1)S(1)} %compare_and_fusion), kind=kOutput, calls=%fused_computation.36 | convolution fusion | flops 50528256 | bytes 1572876 | tf_op jit(solution)/shard_map/ebk,ekf->ebf/dot_general | solution.py:61
  13.1 1.7 %copy.12 = f32[12,128,128]{1,0,2:T(8,128)S(1)} copy(f32[12,128,128]{2,1,0:T(8,128)} %fusion.25) | data formatting | bytes 1572864 | tf_op jit(solution)/shard_map/ebk,ekf->ebf/dot_general | solution.py:61
  15.8 1.0 %pad_maximum_fusion = bf16[4,1,192,512]{3,2,1,0:T(8,128)(2,1)} fusion(bf16[1,1,192,512]{3,2,1,0:T(8,128)(2,1)S(1)} %get-tuple-element.85, bf16[1,1,192,512]{3,2,1,0:T(8,128)(2,1)S(1)} %get-tuple-element.86, bf16[1,1,192,512]{3,2,1,0:T(8,128)(2,1)S(1)} %get-tuple-element.87, bf16[1,1,192,512]{3,2,1,0:T(8,128)(2,1)S(1)} %get-tuple-element.84), kind=kLoop, calls=%fused_computation.33 | loop fusion | flops 1179648 | bytes 1572864 | tf_op jit(solution)/shard_map/stack | solution.py:75
  16.8 4.9 %all-to-all-start = ((bf16[4,1,192,512]{3,2,1,0:T(8,128)(2,1)}), bf16[4,1,192,512]{3,2,1,0:T(8,128)(2,1)S(1)}, u32[]{:S(2)}, u32[]{:S(2)}) async-start(bf16[4,1,192,512]{3,2,1,0:T(8,128)(2,1)} %pad_maximum_fusion), calls=%async_computation | async-start | bytes 1572864 | tf_op jit(solution)/shard_map/all_to_all | solution.py:74
  21.7 21.0 %all-to-all-done = bf16[4,1,192,512]{3,2,1,0:T(8,128)(2,1)S(1)} async-done(((bf16[4,1,192,512]{3,2,1,0:T(8,128)(2,1)}), bf16[4,1,192,512]{3,2,1,0:T(8,128)(2,1)S(1)}, u32[]{:S(2)}, u32[]{:S(2)}) %all-to-all-start) | async-done | bytes 786464 | tf_op jit(solution)/shard_map/all_to_all | solution.py:74
  42.7 4.4 %fusion.20 = f32[4,192,2048]{2,1,0:T(8,128)} fusion(bf16[512,2048]{1,0:T(8,128)(2,1)S(1)} %copy-done, bf16[4,1,192,512]{3,2,1,0:T(8,128)(2,1)S(1)} %all-to-all-done), kind=kOutput, calls=%fused_computation.27 | convolution fusion | flops 1610612736 | bytes 9175040 | tf_op jit(solution)/shard_map/tvp,pg->tvg/dot_general | solution.py:79
  47.1 15.0 %while.15 = (s32[]{:T(128)}, bf16[192,512]{1,0:T(8,128)(2,1)S(1)}, f32[192,512]{1,0:T(8,128)S(1)}, bf16[4,192,512]{2,1,0:T(8,128)(2,1)}, f32[4,192,2048]{2,1,0:T...) while((s32[]{:T(128)}, bf16[192,512]{1,0:T(8,128)(2,1)S(1)}, ...), condition=%wide.region_1.2_spmd.clone, body=%wide.region_0.1_spmd.clone.sunk | while | flops 405110784 | bytes 8200812 | solution.py:91
  47.1 2.6 %fusion.47 = f32[192,2048]{1,0:T(8,128)S(1)} fusion(bf16[512,2048]{1,0:T(8,128)(2,1)} %get-tuple-element.160, f32[4,192,2048]{2,1,0:T(8,128)} %get-tuple-element.159, s32[]{:T(128)} %get-tuple-element.146, f32[2048]{0:T(1024)S(1)} %get-tuple-element.161, bf16[192,512]{1,0:T(8,128)(2,1)S(1)} %get-tuple-element.147, pred[]{:T(512)S(6)} %compare.3), kind=kOutput, calls=%fused_computation.2.clone.1 | convolution fusion | flops 403537920 | bytes 5447685 | tf_op jit(solution)/shard_map/while/body/eval_jaxpr/dot_general | solution.py:28
  49.8 1.1 %bitcast_dynamic-update-slice_fusion.2 = (bf16[4,192,512]{2,1,0:T(8,128)(2,1)}, bf16[192,512]{1,0:T(8,128)(2,1)S(1)}, f32[192,512]{1,0:T(8,128)S(1)}) fusion(bf16[4,192,512]{2,1,0:T(8,128)(2,1)} %get-tuple-element.149, s32[]{:T(128)} %get-tuple-element.146, f32[192,2048]{1,0:T(8,128)S(1)} %fusion.47, f32[192,512]{1,0:T(8,128)S(1)} %get-tuple-element.148, ...), kind=kLoop, calls=%fused_computation.22.clone.1 | loop fusion | flops 1572864 | bytes 2753025 | tf_op jit(solution)/shard_map/while/body/jit(dynamic_update_index_in_dim)/dynamic_update_slice | solution.py:91
  50.9 2.6 %fusion.47 = f32[192,2048]{1,0:T(8,128)S(1)} fusion(bf16[512,2048]{1,0:T(8,128)(2,1)} %get-tuple-element.160, f32[4,192,2048]{2,1,0:T(8,128)} %get-tuple-element.159, s32[]{:T(128)} %get-tuple-element.146, f32[2048]{0:T(1024)S(1)} %get-tuple-element.161, bf16[192,512]{1,0:T(8,128)(2,1)S(1)} %get-tuple-element.147, pred[]{:T(512)S(6)} %compare.3), kind=kOutput, calls=%fused_computation.2.clone.1 | convolution fusion | flops 403537920 | bytes 5447685 | tf_op jit(solution)/shard_map/while/body/eval_jaxpr/dot_general | solution.py:28
  53.5 1.1 %bitcast_dynamic-update-slice_fusion.2 = (bf16[4,192,512]{2,1,0:T(8,128)(2,1)}, bf16[192,512]{1,0:T(8,128)(2,1)S(1)}, f32[192,512]{1,0:T(8,128)S(1)}) fusion(bf16[4,192,512]{2,1,0:T(8,128)(2,1)} %get-tuple-element.149, s32[]{:T(128)} %get-tuple-element.146, f32[192,2048]{1,0:T(8,128)S(1)} %fusion.47, f32[192,512]{1,0:T(8,128)S(1)} %get-tuple-element.148, ...), kind=kLoop, calls=%fused_computation.22.clone.1 | loop fusion | flops 1572864 | bytes 2753025 | tf_op jit(solution)/shard_map/while/body/jit(dynamic_update_index_in_dim)/dynamic_update_slice | solution.py:91
  54.6 2.6 %fusion.47 = f32[192,2048]{1,0:T(8,128)S(1)} fusion(bf16[512,2048]{1,0:T(8,128)(2,1)} %get-tuple-element.160, f32[4,192,2048]{2,1,0:T(8,128)} %get-tuple-element.159, s32[]{:T(128)} %get-tuple-element.146, f32[2048]{0:T(1024)S(1)} %get-tuple-element.161, bf16[192,512]{1,0:T(8,128)(2,1)S(1)} %get-tuple-element.147, pred[]{:T(512)S(6)} %compare.3), kind=kOutput, calls=%fused_computation.2.clone.1 | convolution fusion | flops 403537920 | bytes 5447685 | tf_op jit(solution)/shard_map/while/body/eval_jaxpr/dot_general | solution.py:28
  57.3 1.1 %bitcast_dynamic-update-slice_fusion.2 = (bf16[4,192,512]{2,1,0:T(8,128)(2,1)}, bf16[192,512]{1,0:T(8,128)(2,1)S(1)}, f32[192,512]{1,0:T(8,128)S(1)}) fusion(bf16[4,192,512]{2,1,0:T(8,128)(2,1)} %get-tuple-element.149, s32[]{:T(128)} %get-tuple-element.146, f32[192,2048]{1,0:T(8,128)S(1)} %fusion.47, f32[192,512]{1,0:T(8,128)S(1)} %get-tuple-element.148, ...), kind=kLoop, calls=%fused_computation.22.clone.1 | loop fusion | flops 1572864 | bytes 2753025 | tf_op jit(solution)/shard_map/while/body/jit(dynamic_update_index_in_dim)/dynamic_update_slice | solution.py:91
  58.4 2.6 %fusion.47 = f32[192,2048]{1,0:T(8,128)S(1)} fusion(bf16[512,2048]{1,0:T(8,128)(2,1)} %get-tuple-element.160, f32[4,192,2048]{2,1,0:T(8,128)} %get-tuple-element.159, s32[]{:T(128)} %get-tuple-element.146, f32[2048]{0:T(1024)S(1)} %get-tuple-element.161, bf16[192,512]{1,0:T(8,128)(2,1)S(1)} %get-tuple-element.147, pred[]{:T(512)S(6)} %compare.3), kind=kOutput, calls=%fused_computation.2.clone.1 | convolution fusion | flops 403537920 | bytes 5447685 | tf_op jit(solution)/shard_map/while/body/eval_jaxpr/dot_general | solution.py:28
  61.0 1.1 %bitcast_dynamic-update-slice_fusion.2 = (bf16[4,192,512]{2,1,0:T(8,128)(2,1)}, bf16[192,512]{1,0:T(8,128)(2,1)S(1)}, f32[192,512]{1,0:T(8,128)S(1)}) fusion(bf16[4,192,512]{2,1,0:T(8,128)(2,1)} %get-tuple-element.149, s32[]{:T(128)} %get-tuple-element.146, f32[192,2048]{1,0:T(8,128)S(1)} %fusion.47, f32[192,512]{1,0:T(8,128)S(1)} %get-tuple-element.148, ...), kind=kLoop, calls=%fused_computation.22.clone.1 | loop fusion | flops 1572864 | bytes 2753025 | tf_op jit(solution)/shard_map/while/body/jit(dynamic_update_index_in_dim)/dynamic_update_slice | solution.py:91
  62.1 23.6 %all_to_all.17 = bf16[4,192,512]{2,1,0:T(8,128)(2,1)S(1)} all-to-all(bf16[4,192,512]{2,1,0:T(8,128)(2,1)} %get-tuple-element.42), channel_id=1, replica_groups=mesh['snap'=4,'vert'=8] {'snap'}, dimensions={0} | all-to-all | bytes 1572864 | tf_op jit(solution)/shard_map/all_to_all | solution.py:92
  85.7 0.9 %copy.28 = bf16[1,768,512]{2,1,0:T(8,128)(2,1)} copy(bf16[1,768,512]{2,1,0:T(8,128)(2,1)S(1)} %bitcast.50) | data formatting | bytes 1572864
  (22 shorter events, 1.0 us)
Async XLA Ops:
  0.0 42.7 %copy-start = (bf16[512,2048]{1,0:T(8,128)(2,1)S(1)}, bf16[512,2048]{1,0:T(8,128)(2,1)}, u32[]{:S(2)}) copy-start(bf16[512,2048]{1,0:T(8,128)(2,1)} %param.19) | copy-start | bytes 6291460
  0.0 11.7 %copy-start.1 = (bf16[1,12,128,128]{3,2,1,0:T(8,128)(2,1)S(1)}, bf16[1,12,128,128]{3,2,1,0:T(8,128)(2,1)}, u32[]{:S(2)}) copy-start(bf16[1,12,128,128]{3,2,1,0:T(8,128)(2,1)} %param.13) | copy-start | bytes 1179652
  0.0 8.6 %collective-permute-start = (bf16[1,768,128]{2,1,0:T(8,128)(2,1)}, bf16[1,768,128]{2,1,0:T(8,128)(2,1)S(1)}, u32[]{:S(2)}, u32[]{:S(2)}) collective-permute-start(bf16[1,768,128]{2,1,0:T(8,128)(2,1)} %param.12), channel_id=1, source_target_pairs={{0,1},{1,2},{2,3},{3,4},{4,5},{5,6},{6,7},{8,9},{9,10},{10,11},{11... | collective-permute-start | bytes 589832 | tf_op jit(solution)/shard_map/ppermute | solution.py:17
  2.1 8.0 %collective-permute-start.1 = (bf16[1,768,128]{2,1,0:T(8,128)(2,1)}, bf16[1,768,128]{2,1,0:T(8,128)(2,1)S(1)}, u32[]{:S(2)}, u32[]{:S(2)}) collective-permute-start(bf16[1,768,128]{2,1,0:T(8,128)(2,1)} %param.12), channel_id=1, source_target_pairs={{1,0},{2,1},{3,2},{4,3},{5,4},{6,5},{7,6},{9,8},{10,9},{11,10},{12... | collective-permute-start | bytes 589832 | tf_op jit(solution)/shard_map/ppermute | solution.py:19
  11.7 3.1 %copy-start.5 = (s32[1,12]{1,0:T(1,128)S(1)}, s32[1,12]{1,0:T(1,128)}, u32[]{:S(2)}) copy-start(s32[1,12]{1,0:T(1,128)} %param.15) | copy-start | bytes 148
  13.1 2.2 %copy-start.3 = (bf16[128,512]{1,0:T(8,128)(2,1)S(1)}, bf16[128,512]{1,0:T(8,128)(2,1)}, u32[]{:S(2)}) copy-start(bf16[128,512]{1,0:T(8,128)(2,1)} %param.17) | copy-start | bytes 393220
  13.1 2.2 %copy-start.4 = (f32[512]{0:T(512)S(1)}, f32[512]{0:T(512)}, u32[]{:S(2)}) copy-start(f32[512]{0:T(512)} %param.18) | copy-start | bytes 6148
  16.8 25.9 %all-to-all-start = ((bf16[4,1,192,512]{3,2,1,0:T(8,128)(2,1)}), bf16[4,1,192,512]{3,2,1,0:T(8,128)(2,1)S(1)}, u32[]{:S(2)}, u32[]{:S(2)}) async-start(bf16[4,1,192,512]{3,2,1,0:T(8,128)(2,1)} %pad_maximum_fusion), calls=%async_computation | async-start | bytes 1572864 | tf_op jit(solution)/shard_map/all_to_all | solution.py:74
  21.7 25.5 %copy-start.2 = (f32[2048]{0:T(1024)S(1)}, f32[2048]{0:T(1024)}, u32[]{:S(2)}) copy-start(f32[2048]{0:T(1024)} %param.21) | copy-start | bytes 24580
